TPU v7x, 32 devices: a whole 2x2x4 slice. The times are simulated.
32 devices in a mesh: blocks: 2 (over y), stripe: 4 (over z), cond: 2 (over x), col: 2 (over core).
Axes of the slice: x: 2, y: 2, z: 4, core: 2. Of those that a mesh axis runs over, the one named last changes fastest.
Arguments:
- theta: float32 [1024, 512], P(('blocks', 'stripe', 'cond'), 'col'), parts along dimension 0, may hold values from -6 to 6
- seed_map: int32 [1024, 512], P(('blocks', 'stripe', 'cond'), 'col'), parts along dimension 0, may hold values 0 or 1
- target: bfloat16 [1024, 512], P(('blocks', 'stripe'), 'col'), parts along dimension 0, may hold values from 0 to 1
- row_taps: bfloat16 [5, 6, 129], replicated, may hold values from -0.5 to 0.5
- col_taps: bfloat16 [5, 6, 129], replicated, may hold values from -0.5 to 0.5
- kernel_weight: float32 [5, 6], replicated, may hold values from 0.05 to 0.4
- cond_index: int32 [4], P('cond'), may hold values from 0 to 4
- dose: float32 [4], P('cond'), may hold values from 0.7 to 1.4
Outputs:
- grad_theta: float32 [1024, 512], P(('blocks', 'stripe', 'cond'), 'col'), parts along dimension 0
There are 2 independent parts, one for each index of `blocks`. A program takes and returns all parts, laid end to end along the dimension named above; an argument that names none is the same for every part. Nothing has to cross between parts.
All inputs are finite; a program needn't handle non-finite values. No bound on the sum of `seed_map` on one device may be relied on, other than what follows from the above.
Results may differ from a plain program's by a relative error of at most 0.0059.
Values may be sent and summed in bfloat16 or wider, within the bound.
A program may use at most 64 MiB of HBM per device.

v0:
```python
import jax
import jax.numpy as jnp
from jax import lax
from jax.sharding import PartitionSpec as P

seed_shift = 1.5
steepness = 4.0
threshold = 0.3


def padded(array, sides, width):
    for axis, dim in sides:
        size, length = (lax.axis_size(axis), array.shape[dim])
        up = [(i, (i + 1) % size) for i in range(size - 1)]
        down = [(j, i) for i, j in up]
        last = lax.slice_in_dim(array, length - width, length, axis=dim)
        leading = lax.slice_in_dim(array, 0, width, axis=dim)
        before = lax.ppermute(last, axis, up)
        after = lax.ppermute(leading, axis, down)
        array = jnp.concatenate([before, array, after], axis=dim)
    return array


def band_matrix(tap_table, out_count, in_count, flipped):
    if flipped:
        tap_table = tap_table[..., ::-1]
    leading = tap_table.shape[:-1]
    zero_tail = jnp.zeros(leading + (in_count + 1 - tap_table.shape[-1],), tap_table.dtype)
    period_row = jnp.concatenate([tap_table, zero_tail], axis=-1)
    repeated = jnp.tile(period_row, (1,) * len(leading) + (out_count,))
    return repeated[..., : out_count * in_count].reshape(leading + (out_count, in_count))


def build_bands(row_tap, col_tap, row_ext, band_span):
    own_rows = row_ext - 2 * band_span
    mid_rows = own_rows + band_span
    forward_rows = band_matrix(row_tap, mid_rows, row_ext, False)
    forward_cols = band_matrix(col_tap, band_span, 2 * band_span, False)
    adjoint_cols = band_matrix(col_tap, band_span, 2 * band_span, True)
    adjoint_rows = band_matrix(row_tap, own_rows, mid_rows, True)
    return (forward_rows, forward_cols, adjoint_cols, adjoint_rows)


def block_band(tiles, band_mat, band_span):
    lower = jnp.einsum(
        "kyjp,kqp->kyjq",
        tiles[:, :, :-1],
        band_mat[:, :, :band_span],
        preferred_element_type=jnp.float32,
    )
    upper = jnp.einsum(
        "kyjp,kqp->kyjq",
        tiles[:, :, 1:],
        band_mat[:, :, band_span:],
        preferred_element_type=jnp.float32,
    )
    return lower + upper


def condition_grad(
    ext_mask,
    ext_target,
    valid_area,
    forward_rows,
    forward_cols,
    adjoint_cols,
    adjoint_rows,
    kernel_wt,
    dose_val,
    band_span,
):
    row_ext = ext_mask.shape[0]
    wide_ext = ext_mask.shape[1]
    own_rows = row_ext - 2 * band_span
    mid_rows = own_rows + band_span
    kernel_count = forward_rows.shape[0]
    row_pass = jnp.einsum(
        "kim,mx->kix", forward_rows, ext_mask, preferred_element_type=jnp.float32
    ).astype(jnp.bfloat16)
    blocks_in = wide_ext // band_span
    block_tiles = row_pass.reshape(kernel_count, mid_rows, blocks_in, band_span)
    field_amp = block_band(block_tiles, forward_cols, band_span)
    field_amp = field_amp.reshape(kernel_count, mid_rows, (blocks_in - 1) * band_span)
    intensity = jnp.sum(kernel_wt[:, None, None] * field_amp * field_amp, axis=0)
    resist = jax.nn.sigmoid(steepness * (dose_val * intensity - threshold))
    slope_term = (
        2.0
        * (resist - ext_target.astype(jnp.float32))
        * steepness
        * dose_val
        * resist
        * (1.0 - resist)
    )
    slope_term = jnp.where(valid_area, slope_term, jnp.zeros_like(slope_term))
    dfield = (2.0 * kernel_wt[:, None, None] * field_amp * slope_term[None]).astype(jnp.bfloat16)
    dtiles = dfield.reshape(kernel_count, mid_rows, blocks_in - 1, band_span)
    col_back = block_band(dtiles, adjoint_cols, band_span)
    col_back = col_back.reshape(kernel_count, mid_rows, (blocks_in - 2) * band_span).astype(
        jnp.bfloat16
    )
    return jnp.einsum("kyi,kix->yx", adjoint_rows, col_back, preferred_element_type=jnp.float32)


def valid_span(first_index, count, limit):
    global_index = first_index + jnp.arange(count)
    return (global_index >= 0) & (global_index < limit)


def shards(theta, seed_map, target, row_taps, col_taps, kernel_weight, cond_index, dose):
    half_width = row_taps.shape[2] // 2
    band_span = 2 * half_width
    sig = jax.nn.sigmoid(theta + seed_shift * (2 * seed_map - 1).astype(jnp.float32))
    mask_value = sig.astype(jnp.bfloat16)
    stripe_mask = lax.all_gather(mask_value, "cond", axis=0, tiled=True)
    row_count = stripe_mask.shape[0]
    col_count = stripe_mask.shape[1]
    row_ext = row_count + 2 * band_span
    stacked = jnp.stack([stripe_mask, target])
    focus_count = row_taps.shape[0]
    selector = (cond_index[:, None] == jnp.arange(focus_count)[None, :]).astype(jnp.float32)
    row_sel = jnp.einsum("cf,fkt->ckt", selector, row_taps.astype(jnp.float32)).astype(jnp.bfloat16)
    col_sel = jnp.einsum("cf,fkt->ckt", selector, col_taps.astype(jnp.float32)).astype(jnp.bfloat16)
    weight_sel = jnp.dot(selector, kernel_weight, precision=lax.Precision.HIGHEST)
    cond_count = cond_index.shape[0]
    row_first = lax.axis_index("stripe") * row_count - half_width
    row_valid = valid_span(row_first, row_count + band_span, row_count * lax.axis_size("stripe"))
    extended = padded(stacked, (("stripe", 1), ("col", 2)), band_span)
    col_first = lax.axis_index("col") * col_count - half_width
    col_valid = valid_span(col_first, col_count + band_span, col_count * lax.axis_size("col"))
    valid_area = row_valid[:, None] & col_valid[None, :]
    ext_target = extended[1, half_width:-half_width, half_width:-half_width]
    fwd_rows, fwd_cols, adj_cols, adj_rows = build_bands(row_sel, col_sel, row_ext, band_span)
    grad_total = jnp.zeros((row_count, col_count), jnp.float32)
    for cond_slot in range(cond_count):
        grad_total = grad_total + condition_grad(
            extended[0],
            ext_target,
            valid_area,
            fwd_rows[cond_slot],
            fwd_cols[cond_slot],
            adj_cols[cond_slot],
            adj_rows[cond_slot],
            weight_sel[cond_slot],
            dose[cond_slot],
            band_span,
        )
    owned = lax.psum_scatter(grad_total, "cond", scatter_dimension=0, tiled=True)
    return owned * sig * (1.0 - sig)


def solution(mesh):
    return jax.shard_map(
        shards,
        mesh=mesh,
        in_specs=(
            P(("blocks", "stripe", "cond"), "col"),
            P(("blocks", "stripe", "cond"), "col"),
            P(("blocks", "stripe"), "col"),
            P(),
            P(),
            P(),
            P("cond"),
            P("cond"),
        ),
        out_specs=P(("blocks", "stripe", "cond"), "col"),
        check_vma=False,
    )
```

profile of v0, /device:TPU:0, one launch (start us, length us, event | category | flops | bytes accessed | tf_op | source)
XLA Modules:
  0.0 146.8 jit_solution(7613161917017368992)
XLA Ops:
  6.5 0.9 fusion.36
  7.5 5.5 %all_gather.3 = bf16[128,256]{1,0:T(8,128)(2,1)S(1)} all-gather(bf16[64,256]{1,0:T(8,128)(2,1)S(1)} %fusion.36), channel_id=1, replica_groups=mesh['blocks'=2,'stripe'=4,'cond'=2,'col'=2] {'cond'}, dimensions={0}, use_global_device_ids=true | all-gather | bytes 98304 | tf_op jit(solution)/shard_map/all_gather | solution.py:114
  12.9 1.5 %pad_maximum_fusion.3 = bf16[2,128,256]{2,1,0:T(8,128)(2,1)} fusion(bf16[1,128,256]{2,1,0:T(8,128)(2,1)} %bitcast.157, bf16[1,128,256]{2,1,0:T(8,128)(2,1)S(1)} %bitcast.137), kind=kLoop, calls=%fused_computation.69 | loop fusion | flops 65536 | bytes 262144 | tf_op jit(solution)/shard_map/stack | solution.py:118
  14.4 4.0 %collective-permute-start = (bf16[2,128,256]{2,1,0:T(8,128)(2,1)}, bf16[2,128,256]{2,1,0:T(8,128)(2,1)S(1)}, u32[]{:S(2)}, u32[]{:S(2)}) collective-permute-start(bf16[2,128,256]{2,1,0:T(8,128)(2,1)} %pad_maximum_fusion.3), channel_id=1, source_target_pairs={{0,4},{4,8},{8,12},{1,5},{5,9},{9,13},{2,6},{6,10},{10,14},{3,7},{... | collective-permute-start | bytes 393224 | tf_op jit(solution)/shard_map/ppermute | solution.py:18
  18.5 1.3 collective-permute-start.1
  19.8 0.8 convolution_convert_fusion.3
  20.7 1.9 %tile.18 = bf16[2,6,256,385]{3,2,0,1:T(8,128)(2,1)} broadcast(bf16[2,6,385]{2,0,1:T(2,128)(2,1)S(1)} %concatenate.19), dimensions={0,1,3} | broadcast | bytes 2374680 | tf_op jit(solution)/shard_map/tile | solution.py:30
  22.5 9.2 %tile.19 = bf16[2,6,98560]{2,0,1:T(2,128)(2,1)S(1)} reshape(bf16[2,6,256,385]{3,2,0,1:T(8,128)(2,1)} %tile.18) | data formatting | bytes 4730880 | tf_op jit(solution)/shard_map/tile | solution.py:30
  31.7 26.6 %slice_reduce_fusion.1 = (bf16[6,98304]{1,0:T(8,128)(2,1)}, bf16[6,98304]{1,0:T(8,128)(2,1)}) fusion(bf16[2,6,98560]{2,0,1:T(2,128)(2,1)S(1)} %tile.19), kind=kLoop, calls=%fused_computation.5 | loop fusion | bytes 4718592 | tf_op jit(solution)/shard_map/slice | solution.py:139
  58.4 0.2 convolution_convert_fusion.2
  58.6 0.1 tile.40
  58.7 3.1 %tile.41 = bf16[2,6,32896]{2,0,1:T(2,128)(2,1)S(1)} reshape(bf16[2,6,128,257]{3,2,0,1:T(8,128)(2,1)S(1)} %tile.40) | data formatting | bytes 1579008 | tf_op jit(solution)/shard_map/tile | solution.py:30
  61.8 3.5 %slice_reduce_fusion.6 = (bf16[6,32768]{1,0:T(8,128)(2,1)S(1)}, bf16[6,32768]{1,0:T(8,128)(2,1)S(1)}) fusion(bf16[2,6,32896]{2,0,1:T(2,128)(2,1)S(1)} %tile.41), kind=kLoop, calls=%fused_computation.33 | loop fusion | bytes 1572864 | tf_op jit(solution)/shard_map/slice | solution.py:140
  65.3 0.2 fusion.32
  65.5 0.7 fusion.40
  66.2 0.2 reverse
  66.3 0.1 slice.205
  66.4 0.1 tile.42
  66.6 2.9 %tile.43 = bf16[2,6,32896]{2,0,1:T(2,128)(2,1)S(1)} reshape(bf16[2,6,128,257]{3,2,0,1:T(8,128)(2,1)S(1)} %tile.42) | data formatting | bytes 1579008 | tf_op jit(solution)/shard_map/tile | solution.py:30
  69.5 4.4 %slice_reduce_fusion.5 = (bf16[6,32768]{1,0:T(8,128)(2,1)}, bf16[6,32768]{1,0:T(8,128)(2,1)}) fusion(bf16[2,6,32896]{2,0,1:T(2,128)(2,1)S(1)} %tile.43), kind=kLoop, calls=%fused_computation.32 | loop fusion | bytes 1572864 | tf_op jit(solution)/shard_map/slice | solution.py:141
  73.9 0.2 reverse.1
  74.2 0.1 tile.16
  74.3 3.1 %tile.17 = bf16[2,6,32896]{2,0,1:T(2,128)(2,1)S(1)} reshape(bf16[2,6,128,257]{3,2,0,1:T(8,128)(2,1)S(1)} %tile.16) | data formatting | bytes 1579008 | tf_op jit(solution)/shard_map/tile | solution.py:30
  77.5 4.4 %slice_reduce_fusion.7 = (bf16[6,32768]{1,0:T(8,128)(2,1)}, bf16[6,32768]{1,0:T(8,128)(2,1)}) fusion(bf16[2,6,32896]{2,0,1:T(2,128)(2,1)S(1)} %tile.17), kind=kLoop, calls=%fused_computation.34 | loop fusion | bytes 1572864 | tf_op jit(solution)/shard_map/slice | solution.py:142
  81.9 0.9 copy.139
  82.8 0.8 copy.138
  85.2 1.4 collective-permute-start.2
  86.6 1.3 collective-permute-start.3
  88.0 2.0 %collective-permute-done.3 = bf16[2,384,128]{2,1,0:T(8,128)(2,1)S(1)} collective-permute-done((bf16[2,384,128]{2,1,0:T(8,128)(2,1)S(1)}, bf16[2,384,128]{2,1,0:T(8,128)(2,1)S(1)}, u32[]{:S(2)}, u32[]{:S(2)}) %collective-permute-start.3) | collective-permute-done | bytes 196640 | tf_op jit(solution)/shard_map/ppermute | solution.py:19
  90.0 0.1 pad_maximum_fusion
  90.1 0.6 copy-done.12
  90.6 0.3 copy-done.13
  90.9 2.1 %convolution_convert_fusion.1 = bf16[6,256,512]{2,1,0:T(8,128)(2,1)} fusion(bf16[1,6,256,384]{3,1,2,0:T(8,128)(2,1)S(1)} %bitcast.156, bf16[2,384,512]{2,1,0:T(8,128)(2,1)S(1)} %pad_maximum_fusion), kind=kOutput, calls=%fused_computation.11 | convolution fusion | flops 604766208 | bytes 3538944 | tf_op jit(solution)/shard_map/kim,mx->kix/dot_general | solution.py:77
  93.1 2.4 %reshape.227 = bf16[6,256,4,128]{3,2,1,0:T(4,128)(2,1)S(1)} reshape(bf16[6,256,512]{2,1,0:T(8,128)(2,1)} %convolution_convert_fusion.1) | data formatting | bytes 3145728 | tf_op jit(solution)/shard_map/reshape | solution.py:81
  95.4 1.3 fusion.37
  96.7 0.5 fusion.10
  97.2 0.6 fusion
  97.8 0.8 add_divide_fusion.1
  98.6 0.9 copy.63
  99.5 1.2 copy.64
  100.7 2.0 %and_select_fusion.1 = (f32[1,256,384]{2,1,0:T(8,128)}, bf16[1,256,384]{2,1,0:T(8,128)(2,1)}) fusion(f32[1,256,384]{2,1,0:T(8,128)S(1)} %copy.64, f32[]{:T(128)S(6)} %mul.223, pred[384]{0:T(512)(128)(4,1)S(1)} %fusion.29, pred[256]{0:T(512)(128)(4,1)S(1)} %compare_and_fusion, bf16[2,384,128]{2,1,0:T(8,128)(2,1)} %copy-done.12, ...), kind=kLoop, calls=%fused_computation.37 | loop fusion | flops 1966080 | bytes 1770116 | tf_op jit(solution)/shard_map/jit(_where)/select_n | solution.py:94
  102.6 1.9 %copy.67 = f32[1,256,384]{1,2,0:T(8,128)} copy(f32[1,256,384]{2,1,0:T(8,128)} %get-tuple-element.13) | data formatting | bytes 786432 | tf_op jit(solution)/shard_map/jit(_where)/select_n | solution.py:94
  104.5 1.1 copy.68
  105.7 1.4 fusion.24
  107.2 1.4 add_convert_fusion.1
  108.6 0.5 copy-done.14
  109.1 2.1 %convolution_convert_fusion = bf16[6,256,512]{2,1,0:T(8,128)(2,1)} fusion(bf16[1,6,256,384]{3,1,2,0:T(8,128)(2,1)S(1)} %bitcast.155, bf16[2,384,512]{2,1,0:T(8,128)(2,1)S(1)} %copy-done.14), kind=kOutput, calls=%fused_computation.10 | convolution fusion | flops 604766208 | bytes 3538944 | tf_op jit(solution)/shard_map/kim,mx->kix/dot_general | solution.py:77
  111.2 2.4 %reshape.228 = bf16[6,256,4,128]{3,2,1,0:T(4,128)(2,1)S(1)} reshape(bf16[6,256,512]{2,1,0:T(8,128)(2,1)} %convolution_convert_fusion) | data formatting | bytes 3145728 | tf_op jit(solution)/shard_map/reshape | solution.py:81
  113.6 1.3 fusion.38
  114.8 0.5 fusion.7
  115.3 0.6 fusion.1
  115.9 0.8 add_divide_fusion
  116.7 0.9 copy.72
  117.6 1.2 copy.73
  118.8 0.9 and_select_fusion
  119.7 1.9 %copy.76 = f32[1,256,384]{1,2,0:T(8,128)} copy(f32[1,256,384]{2,1,0:T(8,128)} %and_select_fusion) | data formatting | bytes 786432 | tf_op jit(solution)/shard_map/jit(_where)/select_n | solution.py:94
  121.6 1.1 copy.77
  122.7 0.5 fusion.23
  123.3 0.5 add_convert_fusion
  123.8 0.5 copy-done.5
  124.3 0.4 convolution_bitcast_fusion
  124.7 1.0 fusion.12
  125.8 12.7 %reduce-scatter.2.cloned.1.call-done = f32[64,256]{1,0:T(8,128)} async-done(((f32[128,256]{1,0:T(8,128)}), f32[64,256]{1,0:T(8,128)}) %reduce-scatter.2.cloned.1.call-update) | async-done | bytes 65552 | tf_op jit(solution)/shard_map/reduce_scatter | solution.py:147
  138.5 1.5 %subtract_multiply_fusion = f32[64,256]{1,0:T(8,128)} fusion(f32[64,256]{1,0:T(8,128)} %reduce-scatter.2.cloned.1.call-done, f32[64,256]{1,0:T(8,128)S(1)} %copy-done.16, s32[64,256]{1,0:T(8,128)S(1)} %copy-done.17), kind=kLoop, calls=%fused_computation.70 | loop fusion | flops 180224 | bytes 262144 | tf_op jit(solution)/shard_map/mul | solution.py:148
  (58 shorter events, 0.5 us)
Async XLA Ops:
  6.5 13.3 %copy-start = (bf16[5,6,129]{2,1,0:T(8,128)(2,1)S(1)}, bf16[5,6,129]{2,1,0:T(8,128)(2,1)}, u32[]{:S(2)}) copy-start(bf16[5,6,129]{2,1,0:T(8,128)(2,1)} %param.11) | copy-start | bytes 23224
  6.5 131.9 %reduce-scatter.2.cloned.1.call-start = ((), (), s32[]{:S(2)}) async-start(), calls=%async_computation.1 | async-start | bytes 196608 | tf_op jit(solution)/shard_map/reduce_scatter | solution.py:147
  14.4 70.6 %collective-permute-start = (bf16[2,128,256]{2,1,0:T(8,128)(2,1)}, bf16[2,128,256]{2,1,0:T(8,128)(2,1)S(1)}, u32[]{:S(2)}, u32[]{:S(2)}) collective-permute-start(bf16[2,128,256]{2,1,0:T(8,128)(2,1)} %pad_maximum_fusion.3), channel_id=1, source_target_pairs={{0,4},{4,8},{8,12},{1,5},{5,9},{9,13},{2,6},{6,10},{10,14},{3,7},{... | collective-permute-start | bytes 393224 | tf_op jit(solution)/shard_map/ppermute | solution.py:18
  18.5 66.6 %collective-permute-start.1 = (bf16[2,128,256]{2,1,0:T(8,128)(2,1)}, bf16[2,128,256]{2,1,0:T(8,128)(2,1)S(1)}, u32[]{:S(2)}, u32[]{:S(2)}) collective-permute-start(bf16[2,128,256]{2,1,0:T(8,128)(2,1)} %pad_maximum_fusion.3), channel_id=1, source_target_pairs={{4,0},{8,4},{12,8},{5,1},{9,5},{13,9},{6,2},{10,6},{14,10},{7,3},{... | collective-permute-start | bytes 393224 | tf_op jit(solution)/shard_map/ppermute | solution.py:19
  31.7 26.7 %copy-start.19 = (bf16[5,6,129]{2,1,0:T(8,128)(2,1)S(1)}, bf16[5,6,129]{2,1,0:T(8,128)(2,1)}, u32[]{:S(2)}) copy-start(bf16[5,6,129]{2,1,0:T(8,128)(2,1)} %param.12) | copy-start | bytes 23224
  31.7 26.7 %copy-start.21 = (s32[2]{0:T(128)S(1)}, s32[2]{0:T(128)}, u32[]{:S(2)}) copy-start(s32[2]{0:T(128)} %param.14) | copy-start | bytes 28
  61.8 3.5 %copy-start.20 = (f32[5,6]{1,0:T(8,128)S(1)}, f32[5,6]{1,0:T(8,128)}, u32[]{:S(2)}) copy-start(f32[5,6]{1,0:T(8,128)} %param.13) | copy-start | bytes 364
  61.8 3.7 %copy-start.18 = (f32[2]{0:T(128)S(1)}, f32[2]{0:T(128)}, u32[]{:S(2)}) copy-start(f32[2]{0:T(128)} %param.15) | copy-start | bytes 28
  77.5 4.5 %copy-start.3 = (bf16[6,32768]{1,0:T(8,128)(2,1)S(1)}, bf16[6,32768]{1,0:T(8,128)(2,1)}, u32[]{:S(2)}) copy-start(bf16[6,32768]{1,0:T(8,128)(2,1)} %get-tuple-element.11) | copy-start | bytes 1179652
  81.8 3.1 %copy-start.2 = (bf16[6,32768]{1,0:T(8,128)(2,1)S(1)}, bf16[6,32768]{1,0:T(8,128)(2,1)}, u32[]{:S(2)}) copy-start(bf16[6,32768]{1,0:T(8,128)(2,1)} %get-tuple-element.12) | copy-start | bytes 1179652
  81.9 3.1 %copy-start.10 = (bf16[128,256]{1,0:T(8,128)(2,1)S(1)}, bf16[128,256]{1,0:T(8,128)(2,1)}, u32[]{:S(2)}) copy-start(bf16[128,256]{1,0:T(8,128)(2,1)} %param.10) | copy-start | bytes 196612
  85.0 5.9 %copy-start.9 = (bf16[6,98304]{1,0:T(8,128)(2,1)S(1)}, bf16[6,98304]{1,0:T(8,128)(2,1)}, u32[]{:S(2)}) copy-start(bf16[6,98304]{1,0:T(8,128)(2,1)} %get-tuple-element.5) | copy-start | bytes 3538948
  85.2 2.8 %collective-permute-start.2 = (bf16[2,384,128]{2,1,0:T(8,128)(2,1)S(1)}, bf16[2,384,128]{2,1,0:T(8,128)(2,1)S(1)}, u32[]{:S(2)}, u32[]{:S(2)}) collective-permute-start(bf16[2,384,128]{2,1,0:T(8,128)(2,1)S(1)} %get-tuple-element.19), channel_id=1, source_target_pairs={{0,1},{2,3},{4,5},{6,7},{8,9},{10,11},{12,13},{14,15},{16,17},{18,... | collective-permute-start | bytes 589832 | tf_op jit(solution)/shard_map/ppermute | solution.py:18
  86.6 3.3 %collective-permute-start.3 = (bf16[2,384,128]{2,1,0:T(8,128)(2,1)S(1)}, bf16[2,384,128]{2,1,0:T(8,128)(2,1)S(1)}, u32[]{:S(2)}, u32[]{:S(2)}) collective-permute-start(bf16[2,384,128]{2,1,0:T(8,128)(2,1)S(1)} %get-tuple-element.20), channel_id=1, source_target_pairs={{1,0},{3,2},{5,4},{7,6},{9,8},{11,10},{13,12},{15,14},{17,16},{19,... | collective-permute-start | bytes 589832 | tf_op jit(solution)/shard_map/ppermute | solution.py:19
  88.0 5.1 %copy-start.11 = (bf16[2,384,128]{2,1,0:T(8,128)(2,1)}, bf16[2,384,128]{2,1,0:T(8,128)(2,1)S(1)}, u32[]{:S(2)}) copy-start(bf16[2,384,128]{2,1,0:T(8,128)(2,1)S(1)} %collective-permute-done.2) | copy-start | bytes 589828
  90.0 0.7 copy-start.12
  90.1 0.9 copy-start.13
  105.7 1.5 copy-start.7
  107.2 1.4 copy-start.8
  107.2 1.9 %copy-start.14 = (bf16[2,384,512]{2,1,0:T(8,128)(2,1)S(1)}, bf16[2,384,512]{2,1,0:T(8,128)(2,1)}, u32[]{:S(2)}) copy-start(bf16[2,384,512]{2,1,0:T(8,128)(2,1)} %copy-done.13) | copy-start | bytes 2359300
  113.6 1.3 copy-start.6
  115.9 2.9 %copy-start.15 = (bf16[1,256,384]{2,1,0:T(8,128)(2,1)S(1)}, bf16[1,256,384]{2,1,0:T(8,128)(2,1)}, u32[]{:S(2)}) copy-start(bf16[1,256,384]{2,1,0:T(8,128)(2,1)} %get-tuple-element.14) | copy-start | bytes 589828
  123.2 1.0 copy-start.5
  123.2 1.4 copy-start.1
  123.2 1.4 copy-start.4
  123.8 14.7 %copy-start.16 = (f32[64,256]{1,0:T(8,128)S(1)}, f32[64,256]{1,0:T(8,128)}, u32[]{:S(2)}) copy-start(f32[64,256]{1,0:T(8,128)} %param.8) | copy-start | bytes 196612
  123.8 14.7 %copy-start.17 = (s32[64,256]{1,0:T(8,128)S(1)}, s32[64,256]{1,0:T(8,128)}, u32[]{:S(2)}) copy-start(s32[64,256]{1,0:T(8,128)} %param.9) | copy-start | bytes 196612
Sparse Core Ops, SparseCore 0:
  125.9 12.5 reduce-scatter.1
where the time goes:
time: 148 us; the launch traced here: 147 us
  local copies, waits for them, and re-layouts  82 us (55%)
  between operations  15.2 us (10%)
  waiting for transfers between devices  14.7 us (10%)
  matrix products  12.9 us (9%)
  other arithmetic  8.44 us (6%)
  starting transfers between devices  8.05 us (5%)
  blocking collectives  5.48 us (4%)
    slice x1, local copies, waits for them, and re-layouts, shards(): fwd_rows[cond_slot]  26.6 us
    another operation x8, local copies, waits for them, and re-layouts, band_matrix(): repeated = jnp.tile(period_row, (1,) * len(leading) + (out_count,))  20.5 us
    reduce_scatter x1, waiting for transfers between devices, shards(): lax.psum_scatter(grad_total, 'cond', scatter_dimension=0, tiled=True)  12.7 us
    all_gather x1, blocking collectives, shards(): stripe_mask = lax.all_gather(mask_value, 'cond', axis=0, tiled=True)  5.48 us
    ppermute x2, starting transfers between devices, padded(): before = lax.ppermute(last, axis, up)  5.47 us
    reshape x2, local copies, waits for them, and re-layouts, condition_grad(): block_tiles = row_pass.reshape(kernel_count, mid_rows, blocks_in, band_span)  4.72 us
    slice x1, local copies, waits for them, and re-layouts, shards(): adj_cols[cond_slot]  4.4 us
    slice x1, local copies, waits for them, and re-layouts, shards(): adj_rows[cond_slot]  4.37 us
  transfers between devices with their start and end apart: 5, of which 2 were waited for; matrix products, arithmetic and copies ran while one was open for 43% of the time, Pallas kernels for 0%

commit v1 on v0

--- a/solution.py
+++ b/solution.py
@@ -6,6 +6,25 @@
 seed_shift = 1.5
 steepness = 4.0
 threshold = 0.3
+
+
+def laid_out(pieces, dim):
+    shape = list(pieces.shape[1:])
+    shape[dim] *= pieces.shape[0]
+    return jnp.moveaxis(pieces, 0, dim).reshape(shape)
+
+
+def collected_by_bits(value, axis):
+    count, here = (lax.axis_size(axis), lax.axis_index(axis))
+    parts, distance = (value[None], 1)
+    while distance < count:
+        partner_block = lax.ppermute(parts, axis, [(i, i ^ distance) for i in range(count)])
+        low = here & distance == 0
+        parts = jnp.concatenate(
+            [jnp.where(low, parts, partner_block), jnp.where(low, partner_block, parts)]
+        )
+        distance *= 2
+    return parts
 
 
 def padded(array, sides, width):
@@ -111,7 +130,7 @@
     band_span = 2 * half_width
     sig = jax.nn.sigmoid(theta + seed_shift * (2 * seed_map - 1).astype(jnp.float32))
     mask_value = sig.astype(jnp.bfloat16)
-    stripe_mask = lax.all_gather(mask_value, "cond", axis=0, tiled=True)
+    stripe_mask = laid_out(collected_by_bits(mask_value, "cond"), 0)
     row_count = stripe_mask.shape[0]
     col_count = stripe_mask.shape[1]
     row_ext = row_count + 2 * band_span

time: 148 us -> 143 us (0.966)
  blocking collectives: 5.48 us -> 0 us
  starting transfers between devices: 8.05 us -> 10.5 us
    all_gather x1 -> x0, blocking collectives: 5.48 us -> none  [shards(): stripe_mask = lax.all_gather(mask_value, 'cond', axis=0, tiled=True)]
    ppermute x0 -> x1, starting transfers between devices: none -> 3 us  [collected_by_bits(): lax.ppermute(parts, axis, [(i, i ^ distance) for i in range(count)])]
    reduce_scatter x1, waiting for transfers between devices: 12.7 us -> 9.7 us  [shards(): lax.psum_scatter(grad_total, 'cond', scatter_dimension=0, tiled=True)]
    ppermute x2, waiting for transfers between devices: 2 us -> 4.44 us  [padded(): after = lax.ppermute(leading, axis, down)]
    another operation x1, other arithmetic: 1.5 us -> 0.02 us  [shards(): stacked = jnp.stack([stripe_mask, target])]
  transfers between devices with their start and end apart: 5 -> 6, of which waited for: 2 -> 3; matrix products, arithmetic and copies ran while one was open for 43% -> 45% of each run, Pallas kernels for 0% -> 0%
where the time goes in v1:
time: 143 us; the launch traced here: 142 us
  local copies, waits for them, and re-layouts  81.9 us (57%)
  between operations  15.2 us (11%)
  waiting for transfers between devices  14.2 us (10%)
  matrix products  12.9 us (9%)
  starting transfers between devices  10.5 us (7%)
  other arithmetic  7.67 us (5%)
    slice x1, local copies, waits for them, and re-layouts, shards(): fwd_rows[cond_slot]  26.6 us
    another operation x8, local copies, waits for them, and re-layouts, band_matrix(): repeated = jnp.tile(period_row, (1,) * len(leading) + (out_count,))  20.5 us
    reduce_scatter x1, waiting for transfers between devices, shards(): lax.psum_scatter(grad_total, 'cond', scatter_dimension=0, tiled=True)  9.7 us
    ppermute x2, starting transfers between devices, padded(): before = lax.ppermute(last, axis, up)  4.92 us
    reshape x2, local copies, waits for them, and re-layouts, condition_grad(): block_tiles = row_pass.reshape(kernel_count, mid_rows, blocks_in, band_span)  4.72 us
    ppermute x2, waiting for transfers between devices, padded(): after = lax.ppermute(leading, axis, down)  4.44 us
    slice x1, local copies, waits for them, and re-layouts, shards(): adj_cols[cond_slot]  4.43 us
    slice x1, local copies, waits for them, and re-layouts, shards(): adj_rows[cond_slot]  4.36 us
  transfers between devices with their start and end apart: 6, of which 3 were waited for; matrix products, arithmetic and copies ran while one was open for 45% of the time, Pallas kernels for 0%

profile of v1, /device:TPU:0, one launch (start us, length us, event | category | flops | bytes accessed | tf_op | source)
XLA Modules:
  0.0 142.4 jit_solution(15479500739731341914)
XLA Ops:
  6.5 0.9 convert_bitcast_fusion
  7.5 3.0 %collective-permute-start = (bf16[1,64,256]{2,1,0:T(8,128)(2,1)S(1)}, bf16[1,64,256]{2,1,0:T(8,128)(2,1)}, u32[]{:S(2)}, u32[]{:S(2)}) collective-permute-start(bf16[1,64,256]{2,1,0:T(8,128)(2,1)S(1)} %convert_bitcast_fusion), channel_id=1, source_target_pairs={{0,2},{2,0},{1,3},{3,1},{4,6},{6,4},{5,7},{7,5},{8,10},{10,8},{9,1... | collective-permute-start | bytes 98312 | tf_op jit(solution)/shard_map/ppermute | solution.py:21
  10.5 0.8 convolution_convert_fusion.3
  11.3 1.9 %tile.18 = bf16[2,6,256,385]{3,2,0,1:T(8,128)(2,1)} broadcast(bf16[2,6,385]{2,0,1:T(2,128)(2,1)S(1)} %concatenate.22), dimensions={0,1,3} | broadcast | bytes 2374680 | tf_op jit(solution)/shard_map/tile | solution.py:49
  13.2 9.2 %tile.19 = bf16[2,6,98560]{2,0,1:T(2,128)(2,1)S(1)} reshape(bf16[2,6,256,385]{3,2,0,1:T(8,128)(2,1)} %tile.18) | data formatting | bytes 4730880 | tf_op jit(solution)/shard_map/tile | solution.py:49
  22.4 26.6 %slice_reduce_fusion.1 = (bf16[6,98304]{1,0:T(8,128)(2,1)}, bf16[6,98304]{1,0:T(8,128)(2,1)}) fusion(bf16[2,6,98560]{2,0,1:T(2,128)(2,1)S(1)} %tile.19), kind=kLoop, calls=%fused_computation.5 | loop fusion | bytes 4718592 | tf_op jit(solution)/shard_map/slice | solution.py:158
  49.0 0.2 convolution_convert_fusion.2
  49.2 0.1 tile.40
  49.3 3.1 %tile.41 = bf16[2,6,32896]{2,0,1:T(2,128)(2,1)S(1)} reshape(bf16[2,6,128,257]{3,2,0,1:T(8,128)(2,1)S(1)} %tile.40) | data formatting | bytes 1579008 | tf_op jit(solution)/shard_map/tile | solution.py:49
  52.5 3.5 %slice_reduce_fusion.6 = (bf16[6,32768]{1,0:T(8,128)(2,1)S(1)}, bf16[6,32768]{1,0:T(8,128)(2,1)S(1)}) fusion(bf16[2,6,32896]{2,0,1:T(2,128)(2,1)S(1)} %tile.41), kind=kLoop, calls=%fused_computation.33 | loop fusion | bytes 1572864 | tf_op jit(solution)/shard_map/slice | solution.py:159
  55.9 0.2 fusion.32
  56.1 0.2 reverse
  56.4 0.1 tile.42
  56.6 2.9 %tile.43 = bf16[2,6,32896]{2,0,1:T(2,128)(2,1)S(1)} reshape(bf16[2,6,128,257]{3,2,0,1:T(8,128)(2,1)S(1)} %tile.42) | data formatting | bytes 1579008 | tf_op jit(solution)/shard_map/tile | solution.py:49
  59.5 4.4 %slice_reduce_fusion.5 = (bf16[6,32768]{1,0:T(8,128)(2,1)}, bf16[6,32768]{1,0:T(8,128)(2,1)}) fusion(bf16[2,6,32896]{2,0,1:T(2,128)(2,1)S(1)} %tile.43), kind=kLoop, calls=%fused_computation.32 | loop fusion | bytes 1572864 | tf_op jit(solution)/shard_map/slice | solution.py:160
  63.9 0.2 reverse.1
  64.2 0.1 tile.16
  64.3 3.1 %tile.17 = bf16[2,6,32896]{2,0,1:T(2,128)(2,1)S(1)} reshape(bf16[2,6,128,257]{3,2,0,1:T(8,128)(2,1)S(1)} %tile.16) | data formatting | bytes 1579008 | tf_op jit(solution)/shard_map/tile | solution.py:49
  67.5 4.4 %slice_reduce_fusion.7 = (bf16[6,32768]{1,0:T(8,128)(2,1)}, bf16[6,32768]{1,0:T(8,128)(2,1)}) fusion(bf16[2,6,32896]{2,0,1:T(2,128)(2,1)S(1)} %tile.17), kind=kLoop, calls=%fused_computation.34 | loop fusion | bytes 1572864 | tf_op jit(solution)/shard_map/slice | solution.py:161
  71.9 0.6 fusion.39
  72.5 0.8 broadcast_select_fusion.1
  73.3 3.6 %collective-permute-start.1 = (bf16[2,128,256]{2,1,0:T(8,128)(2,1)S(1)}, bf16[2,128,256]{2,1,0:T(8,128)(2,1)S(1)}, u32[]{:S(2)}, u32[]{:S(2)}) collective-permute-start(bf16[2,128,256]{2,1,0:T(8,128)(2,1)S(1)} %pad_maximum_fusion.3), channel_id=1, source_target_pairs={{0,4},{4,8},{8,12},{1,5},{5,9},{9,13},{2,6},{6,10},{10,14},{3,7},{... | collective-permute-start | bytes 393224 | tf_op jit(solution)/shard_map/ppermute | solution.py:37
  76.9 1.3 collective-permute-start.2
  78.3 0.8 copy.139
  79.1 0.8 copy.138
  81.3 2.4 %collective-permute-done.2 = bf16[2,128,256]{2,1,0:T(8,128)(2,1)S(1)} collective-permute-done((bf16[2,128,256]{2,1,0:T(8,128)(2,1)S(1)}, bf16[2,128,256]{2,1,0:T(8,128)(2,1)S(1)}, u32[]{:S(2)}, u32[]{:S(2)}) %collective-permute-start.2) | collective-permute-done | bytes 131104 | tf_op jit(solution)/shard_map/ppermute | solution.py:38
  83.9 1.3 collective-permute-start.3
  85.2 1.3 collective-permute-start.4
  86.5 2.0 %collective-permute-done.4 = bf16[2,384,128]{2,1,0:T(8,128)(2,1)S(1)} collective-permute-done((bf16[2,384,128]{2,1,0:T(8,128)(2,1)S(1)}, bf16[2,384,128]{2,1,0:T(8,128)(2,1)S(1)}, u32[]{:S(2)}, u32[]{:S(2)}) %collective-permute-start.4) | collective-permute-done | bytes 196640 | tf_op jit(solution)/shard_map/ppermute | solution.py:38
  88.5 0.1 pad_maximum_fusion
  88.6 0.6 copy-done.12
  89.2 0.3 copy-done.13
  89.5 2.1 %convolution_convert_fusion.1 = bf16[6,256,512]{2,1,0:T(8,128)(2,1)} fusion(bf16[1,6,256,384]{3,1,2,0:T(8,128)(2,1)S(1)} %bitcast.158, bf16[2,384,512]{2,1,0:T(8,128)(2,1)S(1)} %pad_maximum_fusion), kind=kOutput, calls=%fused_computation.11 | convolution fusion | flops 604766208 | bytes 3538944 | tf_op jit(solution)/shard_map/kim,mx->kix/dot_general | solution.py:96
  91.6 2.4 %reshape.227 = bf16[6,256,4,128]{3,2,1,0:T(4,128)(2,1)S(1)} reshape(bf16[6,256,512]{2,1,0:T(8,128)(2,1)} %convolution_convert_fusion.1) | data formatting | bytes 3145728 | tf_op jit(solution)/shard_map/reshape | solution.py:100
  94.0 1.3 fusion.36
  95.3 0.5 fusion.10
  95.8 0.6 fusion
  96.4 0.8 add_divide_fusion.1
  97.1 0.9 copy.63
  98.1 1.2 copy.64
  99.2 2.0 %and_select_fusion.1 = (f32[1,256,384]{2,1,0:T(8,128)}, bf16[1,256,384]{2,1,0:T(8,128)(2,1)}) fusion(f32[1,256,384]{2,1,0:T(8,128)S(1)} %copy.64, f32[]{:T(128)S(6)} %mul.223, pred[384]{0:T(512)(128)(4,1)S(1)} %fusion.29, pred[256]{0:T(512)(128)(4,1)S(1)} %compare_and_fusion, bf16[2,384,128]{2,1,0:T(8,128)(2,1)} %copy-done.12, ...), kind=kLoop, calls=%fused_computation.37 | loop fusion | flops 1966080 | bytes 1770116 | tf_op jit(solution)/shard_map/jit(_where)/select_n | solution.py:113
  101.2 1.9 %copy.67 = f32[1,256,384]{1,2,0:T(8,128)} copy(f32[1,256,384]{2,1,0:T(8,128)} %get-tuple-element.13) | data formatting | bytes 786432 | tf_op jit(solution)/shard_map/jit(_where)/select_n | solution.py:113
  103.1 1.1 copy.68
  104.3 1.5 %fusion.24 = f32[6,256,2,128]{1,3,2,0:T(8,128)S(1)} fusion(bf16[6,128,256]{2,1,0:T(8,128)(2,1)} %bitcast.149, f32[6,256,3,128]{3,1,2,0:T(8,128)S(1)} %get-tuple-element.32, f32[256,3,128]{2,0,1:T(8,128)S(1)} %copy.68, f32[6]{0:T(128)S(1)} %get-tuple-element.23), kind=kOutput, calls=%fused_computation.65 | convolution fusion | flops 102432768 | bytes 4522008 | tf_op jit(solution)/shard_map/kyjp,kqp->kyjq/dot_general | solution.py:64
  105.8 1.4 add_convert_fusion.1
  107.2 0.5 copy-done.14
  107.6 2.1 %convolution_convert_fusion = bf16[6,256,512]{2,1,0:T(8,128)(2,1)} fusion(bf16[1,6,256,384]{3,1,2,0:T(8,128)(2,1)S(1)} %bitcast.157, bf16[2,384,512]{2,1,0:T(8,128)(2,1)S(1)} %copy-done.14), kind=kOutput, calls=%fused_computation.10 | convolution fusion | flops 604766208 | bytes 3538944 | tf_op jit(solution)/shard_map/kim,mx->kix/dot_general | solution.py:96
  109.8 2.4 %reshape.228 = bf16[6,256,4,128]{3,2,1,0:T(4,128)(2,1)S(1)} reshape(bf16[6,256,512]{2,1,0:T(8,128)(2,1)} %convolution_convert_fusion) | data formatting | bytes 3145728 | tf_op jit(solution)/shard_map/reshape | solution.py:100
  112.1 1.3 fusion.37
  113.4 0.5 fusion.7
  113.9 0.6 fusion.1
  114.5 0.7 add_divide_fusion
  115.3 0.9 copy.72
  116.2 1.2 copy.73
  117.3 0.9 and_select_fusion
  118.2 1.9 %copy.76 = f32[1,256,384]{1,2,0:T(8,128)} copy(f32[1,256,384]{2,1,0:T(8,128)} %and_select_fusion) | data formatting | bytes 786432 | tf_op jit(solution)/shard_map/jit(_where)/select_n | solution.py:113
  120.1 1.1 copy.77
  121.3 0.5 fusion.23
  121.8 0.5 add_convert_fusion
  122.3 0.5 copy-done.5
  122.8 0.4 convolution_bitcast_fusion
  123.2 1.0 fusion.12
  124.3 9.7 %reduce-scatter.2.cloned.1.call-done = f32[64,256]{1,0:T(8,128)} async-done(((f32[128,256]{1,0:T(8,128)}), f32[64,256]{1,0:T(8,128)}) %reduce-scatter.2.cloned.1.call-update) | async-done | bytes 65552 | tf_op jit(solution)/shard_map/reduce_scatter | solution.py:166
  134.0 1.5 %subtract_multiply_fusion = f32[64,256]{1,0:T(8,128)} fusion(f32[64,256]{1,0:T(8,128)} %reduce-scatter.2.cloned.1.call-done, f32[64,256]{1,0:T(8,128)S(1)} %copy-done.16, s32[64,256]{1,0:T(8,128)S(1)} %copy-done.17), kind=kLoop, calls=%fused_computation.71 | loop fusion | flops 180224 | bytes 262144 | tf_op jit(solution)/shard_map/mul | solution.py:167
  (61 shorter events, 0.6 us)
Async XLA Ops:
  6.5 3.9 %copy-start = (bf16[5,6,129]{2,1,0:T(8,128)(2,1)S(1)}, bf16[5,6,129]{2,1,0:T(8,128)(2,1)}, u32[]{:S(2)}) copy-start(bf16[5,6,129]{2,1,0:T(8,128)(2,1)} %param.11) | copy-start | bytes 23224
  6.5 127.5 %reduce-scatter.2.cloned.1.call-start = ((), (), s32[]{:S(2)}) async-start(), calls=%async_computation.1 | async-start | bytes 196608 | tf_op jit(solution)/shard_map/reduce_scatter | solution.py:166
  7.5 65.0 %collective-permute-start = (bf16[1,64,256]{2,1,0:T(8,128)(2,1)S(1)}, bf16[1,64,256]{2,1,0:T(8,128)(2,1)}, u32[]{:S(2)}, u32[]{:S(2)}) collective-permute-start(bf16[1,64,256]{2,1,0:T(8,128)(2,1)S(1)} %convert_bitcast_fusion), channel_id=1, source_target_pairs={{0,2},{2,0},{1,3},{3,1},{4,6},{6,4},{5,7},{7,5},{8,10},{10,8},{9,1... | collective-permute-start | bytes 98312 | tf_op jit(solution)/shard_map/ppermute | solution.py:21
  22.4 26.7 %copy-start.19 = (bf16[5,6,129]{2,1,0:T(8,128)(2,1)S(1)}, bf16[5,6,129]{2,1,0:T(8,128)(2,1)}, u32[]{:S(2)}) copy-start(bf16[5,6,129]{2,1,0:T(8,128)(2,1)} %param.12) | copy-start | bytes 23224
  22.4 26.7 %copy-start.21 = (s32[2]{0:T(128)S(1)}, s32[2]{0:T(128)}, u32[]{:S(2)}) copy-start(s32[2]{0:T(128)} %param.14) | copy-start | bytes 28
  52.5 3.5 %copy-start.20 = (f32[5,6]{1,0:T(8,128)S(1)}, f32[5,6]{1,0:T(8,128)}, u32[]{:S(2)}) copy-start(f32[5,6]{1,0:T(8,128)} %param.13) | copy-start | bytes 364
  67.5 4.4 %copy-start.18 = (f32[2]{0:T(128)S(1)}, f32[2]{0:T(128)}, u32[]{:S(2)}) copy-start(f32[2]{0:T(128)} %param.15) | copy-start | bytes 28
  67.5 5.8 %copy-start.10 = (bf16[128,256]{1,0:T(8,128)(2,1)S(1)}, bf16[128,256]{1,0:T(8,128)(2,1)}, u32[]{:S(2)}) copy-start(bf16[128,256]{1,0:T(8,128)(2,1)} %param.10) | copy-start | bytes 196612
  67.5 10.8 %copy-start.3 = (bf16[6,32768]{1,0:T(8,128)(2,1)S(1)}, bf16[6,32768]{1,0:T(8,128)(2,1)}, u32[]{:S(2)}) copy-start(bf16[6,32768]{1,0:T(8,128)(2,1)} %get-tuple-element.11) | copy-start | bytes 1179652
  73.2 8.0 %copy-start.2 = (bf16[6,32768]{1,0:T(8,128)(2,1)S(1)}, bf16[6,32768]{1,0:T(8,128)(2,1)}, u32[]{:S(2)}) copy-start(bf16[6,32768]{1,0:T(8,128)(2,1)} %get-tuple-element.12) | copy-start | bytes 1179652
  73.3 8.0 %collective-permute-start.1 = (bf16[2,128,256]{2,1,0:T(8,128)(2,1)S(1)}, bf16[2,128,256]{2,1,0:T(8,128)(2,1)S(1)}, u32[]{:S(2)}, u32[]{:S(2)}) collective-permute-start(bf16[2,128,256]{2,1,0:T(8,128)(2,1)S(1)} %pad_maximum_fusion.3), channel_id=1, source_target_pairs={{0,4},{4,8},{8,12},{1,5},{5,9},{9,13},{2,6},{6,10},{10,14},{3,7},{... | collective-permute-start | bytes 393224 | tf_op jit(solution)/shard_map/ppermute | solution.py:37
  76.9 6.9 %collective-permute-start.2 = (bf16[2,128,256]{2,1,0:T(8,128)(2,1)S(1)}, bf16[2,128,256]{2,1,0:T(8,128)(2,1)S(1)}, u32[]{:S(2)}, u32[]{:S(2)}) collective-permute-start(bf16[2,128,256]{2,1,0:T(8,128)(2,1)S(1)} %pad_maximum_fusion.3), channel_id=1, source_target_pairs={{4,0},{8,4},{12,8},{5,1},{9,5},{13,9},{6,2},{10,6},{14,10},{7,3},{... | collective-permute-start | bytes 393224 | tf_op jit(solution)/shard_map/ppermute | solution.py:38
  81.3 8.2 %copy-start.9 = (bf16[6,98304]{1,0:T(8,128)(2,1)S(1)}, bf16[6,98304]{1,0:T(8,128)(2,1)}, u32[]{:S(2)}) copy-start(bf16[6,98304]{1,0:T(8,128)(2,1)} %get-tuple-element.5) | copy-start | bytes 3538948
  83.9 2.6 %collective-permute-start.3 = (bf16[2,384,128]{2,1,0:T(8,128)(2,1)S(1)}, bf16[2,384,128]{2,1,0:T(8,128)(2,1)S(1)}, u32[]{:S(2)}, u32[]{:S(2)}) collective-permute-start(bf16[2,384,128]{2,1,0:T(8,128)(2,1)S(1)} %get-tuple-element.19), channel_id=1, source_target_pairs={{0,1},{2,3},{4,5},{6,7},{8,9},{10,11},{12,13},{14,15},{16,17},{18,... | collective-permute-start | bytes 589832 | tf_op jit(solution)/shard_map/ppermute | solution.py:37
  85.2 3.3 %collective-permute-start.4 = (bf16[2,384,128]{2,1,0:T(8,128)(2,1)S(1)}, bf16[2,384,128]{2,1,0:T(8,128)(2,1)S(1)}, u32[]{:S(2)}, u32[]{:S(2)}) collective-permute-start(bf16[2,384,128]{2,1,0:T(8,128)(2,1)S(1)} %get-tuple-element.20), channel_id=1, source_target_pairs={{1,0},{3,2},{5,4},{7,6},{9,8},{11,10},{13,12},{15,14},{17,16},{19,... | collective-permute-start | bytes 589832 | tf_op jit(solution)/shard_map/ppermute | solution.py:38
  86.5 5.1 %copy-start.11 = (bf16[2,384,128]{2,1,0:T(8,128)(2,1)}, bf16[2,384,128]{2,1,0:T(8,128)(2,1)S(1)}, u32[]{:S(2)}) copy-start(bf16[2,384,128]{2,1,0:T(8,128)(2,1)S(1)} %collective-permute-done.3) | copy-start | bytes 589828
  88.5 0.7 copy-start.12
  88.6 0.9 copy-start.13
  104.3 1.5 %copy-start.7 = (bf16[1,6,128,256]{3,2,1,0:T(8,128)(2,1)S(1)}, bf16[1,6,128,256]{3,2,1,0:T(8,128)(2,1)}, u32[]{:S(2)}) copy-start(bf16[1,6,128,256]{3,2,1,0:T(8,128)(2,1)} %copy.139) | copy-start | bytes 1179652
  105.8 1.4 copy-start.8
  105.8 1.9 %copy-start.14 = (bf16[2,384,512]{2,1,0:T(8,128)(2,1)S(1)}, bf16[2,384,512]{2,1,0:T(8,128)(2,1)}, u32[]{:S(2)}) copy-start(bf16[2,384,512]{2,1,0:T(8,128)(2,1)} %copy-done.13) | copy-start | bytes 2359300
  112.1 1.3 copy-start.6
  114.5 2.8 %copy-start.15 = (bf16[1,256,384]{2,1,0:T(8,128)(2,1)S(1)}, bf16[1,256,384]{2,1,0:T(8,128)(2,1)}, u32[]{:S(2)}) copy-start(bf16[1,256,384]{2,1,0:T(8,128)(2,1)} %get-tuple-element.14) | copy-start | bytes 589828
  121.8 1.0 copy-start.5
  121.8 1.4 %copy-start.1 = (bf16[6,256,2,128]{1,3,2,0:T(8,128)(2,1)S(1)}, bf16[6,256,2,128]{1,3,2,0:T(8,128)(2,1)}, u32[]{:S(2)}) copy-start(bf16[6,256,2,128]{1,3,2,0:T(8,128)(2,1)} %add_convert_fusion.1) | copy-start | bytes 2359300
  121.8 1.4 %copy-start.4 = (bf16[6,32768]{1,0:T(8,128)(2,1)S(1)}, bf16[6,32768]{1,0:T(8,128)(2,1)}, u32[]{:S(2)}) copy-start(bf16[6,32768]{1,0:T(8,128)(2,1)} %get-tuple-element.7) | copy-start | bytes 1179652
  122.3 11.7 %copy-start.16 = (f32[64,256]{1,0:T(8,128)S(1)}, f32[64,256]{1,0:T(8,128)}, u32[]{:S(2)}) copy-start(f32[64,256]{1,0:T(8,128)} %param.8) | copy-start | bytes 196612
  122.3 11.7 %copy-start.17 = (s32[64,256]{1,0:T(8,128)S(1)}, s32[64,256]{1,0:T(8,128)}, u32[]{:S(2)}) copy-start(s32[64,256]{1,0:T(8,128)} %param.9) | copy-start | bytes 196612
Sparse Core Ops, SparseCore 0:
  124.4 9.5 reduce-scatter.1
